TPU v7x, 32 devices: a whole 2x2x4 slice. The times are simulated.
32 devices in a mesh: expert: 8 (over z, y), dp: 4 (over x, core).
Axes of the slice: x: 2, y: 2, z: 4, core: 2. Of those that a mesh axis runs over, the one named last changes fastest.
Arguments:
- features: bfloat16 [32, 3072, 256], P(('expert', 'dp')), may hold values from -6 to 6
- expert_of: int32 [32, 3072, 1], P(('expert', 'dp')), may hold values from 0 to 127, as said below
- segment_of: int32 [32, 3072], P(('expert', 'dp')), may hold values from 0 to 47, never falling along the last dimension, each value on 1 to 128 neighbouring positions
- step_len: float32 [32, 3072], P(('expert', 'dp')), may hold values from 0.005 to 0.05
- target: float32 [32, 3072], P(('expert', 'dp')), may hold values from -6 to 6
- w_first: bfloat16 [128, 256, 256], P(('expert', 'dp')), may hold values from -0.375 to 0.375
- w_second: bfloat16 [128, 256, 256], P(('expert', 'dp')), may hold values from -0.375 to 0.375
- w_head: bfloat16 [128, 256], P(('expert', 'dp')), may hold values from -1.25 to 1.25
Outputs:
- extinction: float32 [32, 3072], P(('expert', 'dp'))
- grad_first: bfloat16 [128, 256, 256], P(('expert', 'dp'))
- grad_second: bfloat16 [128, 256, 256], P(('expert', 'dp'))
- grad_head: bfloat16 [128, 256], P(('expert', 'dp'))
Inputs may be any that keep to these rules, and one draw needn't show every extreme that they name: `expert_of`: experts e * 4 to e * 4 + 3 lie on device e. On every device, no expert is named by more than 48 samples and one is named by exactly 48; the experts of no one device are named by more than 144 samples together, and those of one device by exactly 144. `segment_of`: within a device, sightline numbers never fall along the samples; each sightline has 1 to 128 samples and one has exactly 128.
All inputs are finite; a program needn't handle non-finite values.
Results may differ from a plain program's by a relative error of at most 0.0059.
Values may be sent and summed in bfloat16 or wider, within the bound.
A program may use at most 128 MiB of HBM per device.

v0:
```python
import functools

import jax
import jax.numpy as jnp
from jax import lax
from jax.experimental import pallas as pl
from jax.experimental.pallas import tpu as pltpu
from jax.sharding import PartitionSpec as P

MESH = pl.DeviceIdType.MESH
ROWS = 8


def up(value, unit):
    return (value + unit - 1) // unit * unit


def nt(a, b):
    return lax.dot_general(a, b, (((1,), (1,)), ((), ())), preferred_element_type=jnp.float32)


def tn(a, b):
    return lax.dot_general(a, b, (((0,), (0,)), ((), ())), preferred_element_type=jnp.float32)


def nn(a, b):
    return jnp.dot(a, b, preferred_element_type=jnp.float32)


def split2(x):
    high = x.astype(jnp.bfloat16)
    low = (x - high.astype(jnp.float32)).astype(jnp.bfloat16)
    return high, low


def one(mask):
    return jnp.where(mask, 1.0, 0.0).astype(jnp.bfloat16)


def kernel(
    cfg,
    feat, eof, seg, step, targ, w1, w2, wh,
    ext_o, g1_o, g2_o, gh_o,
    own_s, oh_s, slot_s, rank_s,
    send, recv, msend, mrecv,
    x_s, a1_s, a2_s, sl1_s, hs2_s, gp2_s,
    dens, sig, table, tcol, grads, gsend, grecv, row_s, fore_s, back_s,
    fss, frs, mss, mrs, dss, drs, gss, grs,
):
    NE, ND, EL, S, NB, cap, dcp, G, CH = cfg
    D = NE * ND
    Q = D * ROWS
    NG = D // G
    GR = G * cap
    SPC = CH * G
    NCH = NG // CH
    CR = CH * GR
    nblk = S // NB
    lgn = NE.bit_length() - 1
    keep = D <= 64
    e_me = lax.axis_index("expert")
    d_me = lax.axis_index("dp")

    def shifts(j):
        return NE - 1 - lax.rem(j, NE), ND - 1 - j // NE

    def to_dev(j):
        ke, kd = shifts(j)
        return (lax.rem(e_me + ke, NE), lax.rem(d_me + kd, ND))

    def from_dev(j):
        ke, kd = shifts(j)
        return (lax.rem(e_me - ke + NE, NE), lax.rem(d_me - kd + ND, ND))

    barrier = pltpu.get_barrier_semaphore()

    def greet(j, c):
        pl.semaphore_signal(barrier, inc=1, device_id=to_dev(j), device_id_type=MESH)
        return c

    lax.fori_loop(0, D - 1, greet, 0)

    def loop(n, body, init):
        if not keep:
            return lax.fori_loop(0, n, body, init)
        for b in range(n):
            init = body(b, init)
        return init

    qi = lax.broadcasted_iota(jnp.int32, (Q, NB), 0)
    jq = qi >> 3
    mq = qi & (ROWS - 1)
    de = (e_me + (NE - 1 - (jq & (NE - 1)))) & (NE - 1)
    dd = (d_me + (ND - 1 - (jq >> lgn))) & (ND - 1)
    own_s[...] = jnp.where(mq < EL, (de * ND + dd) * EL + mq, -1)

    tri = lax.broadcasted_iota(jnp.int32, (NB, NB + 128), 0) < lax.broadcasted_iota(
        jnp.int32, (NB, NB + 128), 1
    )
    tri = one(jnp.logical_or(tri, lax.broadcasted_iota(jnp.int32, (NB, NB + 128), 1) >= NB))

    def cols(b):
        return pl.ds(b * NB if keep else pl.multiple_of(b * NB, NB), NB)

    def tile(x):
        return jnp.concatenate([x] * (NB // 128), axis=1)

    def hot(b):
        if keep:
            return oh_s[:, cols(b)]
        return one(eof[:, cols(b)] == own_s[...])

    def rank_pass(b, carry):
        hit = eof[:, cols(b)] == own_s[...]
        hits = one(hit)
        if keep:
            oh_s[:, cols(b)] = hits
        full = nn(hits, tri)
        ranks = full[:, :NB] + tile(carry)
        rank_s[:, cols(b)] = jnp.sum(jnp.where(hit, ranks, 0.0), axis=0, keepdims=True)
        return carry + full[:, NB:]

    counts = loop(nblk, rank_pass, jnp.zeros((Q, 128), jnp.float32))
    q128 = lax.broadcasted_iota(jnp.int32, (Q, 128), 0)
    ends = counts
    for t in range(1, EL):
        ends = ends + jnp.where((q128 & (ROWS - 1)) >= t, pltpu.roll(counts, t, 0), 0.0)
    msend[...] = ends.reshape(D, ROWS, 128)[:, :EL, :]
    base = ((q128 >> 3) * dcp).astype(jnp.float32) + ends - counts
    shift = (((q128 >> 3) & (G - 1)) * cap).astype(jnp.float32)

    def slot_pass(b, c):
        hit = eof[:, cols(b)] == own_s[...]
        rank = rank_s[:, cols(b)]
        at = jnp.sum(jnp.where(hit, tile(base), 0.0), axis=0, keepdims=True) + rank
        slot_s[:, cols(b)] = at.astype(jnp.int32)
        if G > 1:
            rank_s[:, cols(b)] = rank + jnp.sum(
                jnp.where(hit, tile(shift), 0.0), axis=0, keepdims=True
            )
        return c

    loop(nblk, slot_pass, 0)

    pl.semaphore_wait(barrier, D - 1)

    def frows(j):
        return pl.ds(pl.multiple_of(j * dcp, dcp), dcp)

    def meta_copy(j, c):
        pltpu.make_async_remote_copy(
            src_ref=msend.at[j], dst_ref=mrecv.at[j], send_sem=mss, recv_sem=mrs,
            device_id=to_dev(j), device_id_type=MESH,
        ).start()
        return c

    lax.fori_loop(0, D - 1, meta_copy, 0)
    pltpu.make_async_copy(msend.at[D - 1], mrecv.at[D - 1], mrs).start()

    def feature_copy(j):
        pltpu.make_async_remote_copy(
            src_ref=send.at[frows(j)], dst_ref=recv.at[frows(j)],
            send_sem=fss, recv_sem=frs.at[j // SPC],
            device_id=to_dev(j), device_id_type=MESH,
        ).start()

    PK = 2
    PR = PK * dcp

    def pack(p):
        acc = None
        for b in range(S // 256):
            s = slice(b * 256, (b + 1) * 256)
            want = lax.broadcasted_iota(jnp.int32, (PR, 256), 0)
            part = nn(one((slot_s[:, s] - p * PR) == want), feat[0, s, :])
            acc = part if acc is None else acc + part
        send[pl.ds(pl.multiple_of(p * PR, PR), PR), :] = acc.astype(jnp.bfloat16)

    def pack_send(p, c):
        pack(p)

        feature_copy(p * PK)

        @pl.when(p < D // PK - 1)
        def _():
            feature_copy(p * PK + 1)

        @pl.when(p == D // PK - 1)
        def _():
            mine = frows(D - 1)
            pltpu.make_async_copy(send.at[mine], recv.at[mine], frs.at[NCH - 1]).start()

        return c

    lax.fori_loop(0, D // PK, pack_send, 0)

    wide = (ROWS, S)
    segs = jnp.broadcast_to(seg[...], wide)
    pos = lax.broadcasted_iota(jnp.int32, wide, 1)
    fore = jnp.ones(wide, jnp.float32)
    back = fore
    for k in range(7):
        s = 1 << k
        same = jnp.logical_and(pltpu.roll(segs, s, 1) == segs, pos >= s)
        fore = fore + jnp.where(same, pltpu.roll(fore, s, 1), 0.0)
        same = jnp.logical_and(pltpu.roll(segs, S - s, 1) == segs, pos < S - s)
        back = back + jnp.where(same, pltpu.roll(back, S - s, 1), 0.0)
    fore_s[...] = fore
    back_s[...] = back

    pltpu.make_async_copy(mrecv, mrecv, mrs).wait()

    lane = lax.broadcasted_iota(jnp.int32, (1, G * dcp), 1)
    lane_g = lane // dcp if G > 1 else None
    lane_j = (lane - lane_g * dcp if G > 1 else lane).astype(jnp.float32)
    sub8 = lax.broadcasted_iota(jnp.int32, (ROWS, 1), 0)

    def forward(ci, c):
        span = pl.ds(pl.multiple_of(ci * SPC * dcp, SPC * dcp), SPC * dcp)
        pltpu.make_async_copy(recv.at[span], recv.at[span], frs.at[ci]).wait()
        for g in range(CH):
            grp = ci * CH + g
            targets = [jnp.full((1, G * dcp), -1.0, jnp.float32) for _ in range(EL)]
            for h in range(G):
                m = mrecv[grp * G + h]
                for e in range(EL):
                    lo = m[e - 1 : e, 0:1] if e else jnp.zeros((1, 1), jnp.float32)
                    hi = m[e : e + 1, 0:1]
                    ok = jnp.logical_and(lane_j >= lo, lane_j < hi)
                    if G > 1:
                        ok = jnp.logical_and(ok, lane_g == h)
                    targets[e] = jnp.where(ok, lane_j - lo + h * cap, targets[e])
            want = lax.broadcasted_iota(jnp.int32, (GR, G * dcp), 0).astype(jnp.float32)
            pick = jnp.concatenate([one(t == want) for t in targets], axis=0)
            rows = recv[pl.ds(pl.multiple_of(grp * G * dcp, G * dcp), G * dcp), :]
            x = nn(pick, rows).astype(jnp.bfloat16)
            for e in range(EL):
                x_s[e, pl.ds(pl.multiple_of(grp * GR, GR), GR), :] = x[e * GR : (e + 1) * GR]
        own = pl.ds(pl.multiple_of(ci * CR, CR), CR)
        logit = []
        for e in range(EL):
            p1 = nn(x_s[e, own, :], w1[e])
            s1 = jax.nn.sigmoid(p1)
            a1 = (p1 * s1).astype(jnp.bfloat16)
            a1_s[e, own, :] = a1
            sl1_s[e, own, :] = s1 * (1.0 + p1 * (1.0 - s1))
            p2 = nn(a1, w2[e])
            s2 = jax.nn.sigmoid(p2)
            a2 = (p2 * s2).astype(jnp.bfloat16)
            a2_s[e, own, :] = a2
            head = wh[e : e + 1, :]
            hs2_s[e, own, :] = head.astype(jnp.float32) * (s2 * (1.0 + p2 * (1.0 - s2)))
            logit.append(nt(jnp.broadcast_to(head, (16, head.shape[1])), a2)[:ROWS])
        lg = jnp.zeros((ROWS, CR), jnp.float32)
        for e in range(EL):
            lg = jnp.where(sub8 == e, logit[e], lg)
        den = jnp.maximum(lg, 0.0) + jnp.log1p(jnp.exp(-jnp.abs(lg)))
        sg = jax.nn.sigmoid(lg)
        pad = jnp.zeros((ROWS, 128 - GR), jnp.float32)
        for g in range(CH):
            grp = ci * CH + g
            dens[grp] = jnp.concatenate([den[:, g * GR : (g + 1) * GR], pad], axis=1)[:EL]
            sig[grp] = jnp.concatenate([sg[:, g * GR : (g + 1) * GR], pad], axis=1)

        def give(j, c2):
            @pl.when(j == D - 1)
            def _():
                pltpu.make_async_copy(dens.at[NG - 1], table.at[D - 1], drs).start()

            @pl.when(j < D - 1)
            def _():
                pltpu.make_async_remote_copy(
                    src_ref=dens.at[j // G], dst_ref=table.at[j], send_sem=dss, recv_sem=drs,
                    device_id=from_dev(j), device_id_type=MESH,
                ).start()

            return c2

        lax.fori_loop(ci * SPC, (ci + 1) * SPC, give, 0)
        return c

    lax.fori_loop(0, NCH, forward, 0)

    grads[...] = jnp.zeros_like(grads)
    pltpu.make_async_copy(table, table, drs).wait()
    grads[:, 0:EL, :] = table[...]
    tt = grads[...].reshape(Q, 128).T[:GR]
    th, tl = split2(tt)
    tcol[0:GR, :] = th
    tcol[GR : 2 * GR, :] = tl

    def spread(b, c):
        both = nn(tcol[...], hot(b))
        both = both[:GR] + both[GR:]
        want = lax.broadcasted_iota(jnp.int32, (GR, NB), 0).astype(jnp.float32)
        row_s[:, cols(b)] = jnp.sum(
            jnp.where(rank_s[:, cols(b)] == want, both, 0.0), axis=0, keepdims=True
        )
        return c

    loop(nblk, spread, 0)

    steps = jnp.broadcast_to(step[...], wide)
    run = jnp.broadcast_to(row_s[...], wide) * steps
    before = fore_s[...]
    for k in range(7):
        s = 1 << k
        run = run + jnp.where(before > s, pltpu.roll(run, s, 1), 0.0)
    ext_o[...] = run[0:1]
    run = run - jnp.broadcast_to(targ[...], wide)
    after = back_s[...]
    for k in range(7):
        s = 1 << k
        run = run + jnp.where(after > s, pltpu.roll(run, S - s, 1), 0.0)
    row_s[...] = (run * steps)[0:1]

    def collect(b, total):
        want = lax.broadcasted_iota(jnp.int32, (GR, NB), 0).astype(jnp.float32)
        held = jnp.where(rank_s[:, cols(b)] == want, row_s[:, cols(b)], 0.0)
        both = jnp.concatenate(split2(held), axis=0)
        return total + nt(hot(b), both)

    got = loop(nblk, collect, jnp.zeros((Q, 2 * GR), jnp.float32))
    got = got[:, :GR] + got[:, GR:]
    got = jnp.concatenate([got, jnp.zeros((Q, 128 - GR), jnp.float32)], axis=1)
    gsend[...] = got.reshape(D, ROWS, 128)[:, :EL, :]

    pltpu.make_async_copy(gsend.at[D - 1], grecv.at[D - 1], grs).start()

    def grad_copy(j, c):
        pltpu.make_async_remote_copy(
            src_ref=gsend.at[j], dst_ref=grecv.at[j], send_sem=gss, recv_sem=grs,
            device_id=to_dev(j), device_id_type=MESH,
        ).start()
        return c

    lax.fori_loop(0, D - 1, grad_copy, 0)
    pltpu.make_async_copy(grecv, grecv, grs).wait()

    wid = w1.shape[2]

    def scale(ci, accs):
        parts = []
        for g in range(CH):
            grp = ci * CH + g
            tot = grecv[grp * G]
            for h in range(1, G):
                tot = tot + grecv[grp * G + h]
            parts.append(jnp.concatenate([tot, tot], axis=0)[:ROWS] * sig[grp])
        gt = jnp.concatenate(parts, axis=0).T[:GR]
        out = []
        for e in range(EL):
            acc = accs[e]
            for g in range(CH):
                rows = pl.ds(pl.multiple_of((ci * CH + g) * GR, GR), GR)
                q = g * ROWS + e
                col = gt[:, q : q + 1]
                gp2_s[e, rows, :] = (col * hs2_s[e, rows, :]).astype(jnp.bfloat16)
                colb = col.astype(jnp.bfloat16).astype(jnp.float32)
                acc = acc + colb * a2_s[e, rows, :].astype(jnp.float32)
            out.append(acc)
        return tuple(out)

    accs = lax.fori_loop(
        0, NCH, scale, tuple(jnp.zeros((GR, wid), jnp.float32) for _ in range(EL))
    )
    for e in range(EL):
        gh_o[e : e + 1, :] = jnp.sum(accs[e], axis=0, keepdims=True).astype(jnp.bfloat16)

    def weights(e, c):
        gp2 = gp2_s[e]
        g2_o[e] = tn(a1_s[e], gp2).astype(jnp.bfloat16)
        gp1 = (nt(gp2, w2[e]) * sl1_s[e]).astype(jnp.bfloat16)
        g1_o[e] = tn(x_s[e], gp1).astype(jnp.bfloat16)
        return c

    for e in range(EL):
        weights(e, 0)

    sent = pl.ds(0, (D - 1) * dcp)
    pltpu.make_async_copy(send.at[sent], send.at[sent], fss).wait()
    rest = pl.ds(0, D - 1)
    pltpu.make_async_copy(msend.at[rest], msend.at[rest], mss).wait()
    pltpu.make_async_copy(table.at[rest], table.at[rest], dss).wait()
    pltpu.make_async_copy(gsend.at[rest], gsend.at[rest], gss).wait()


def hand_on(*refs):
    half = len(refs) // 2
    for source, to in zip(refs[:half], refs[half:]):
        to[...] = source[...]


def local(ne, nd, features, expert_of, segment_of, step_len, target, w_first, w_second, w_head):
    EL, F, H = w_first.shape
    S = features.shape[1]
    D = ne * nd
    cap = max(3, (2 * S + D * EL - 1) // (D * EL))
    dcp = up(3 * cap, 16)
    G = 1 if cap % 16 == 0 else 16
    NG = D // G
    CH = 4 if NG % 4 == 0 else 1
    NCH = NG // CH
    NB = 256 if D <= 64 else 128
    GR = G * cap
    Q = D * ROWS
    cfg = (ne, nd, EL, S, NB, cap, dcp, G, CH)
    bf, f32, i32 = jnp.bfloat16, jnp.float32, jnp.int32
    V = pltpu.VMEM
    dma = pltpu.SemaphoreType.DMA
    R = NG * GR
    vm = pl.BlockSpec(memory_space=pltpu.VMEM)
    outs = pl.pallas_call(
        functools.partial(kernel, cfg),
        out_shape=(
            jax.ShapeDtypeStruct((1, S), f32),
            jax.ShapeDtypeStruct((EL, F, H), bf),
            jax.ShapeDtypeStruct((EL, H, H), bf),
            jax.ShapeDtypeStruct((EL, H), bf),
        ),
        in_specs=[vm] * 8,
        out_specs=(vm,) * 4,
        scratch_shapes=[
            V((Q, NB), i32), V((Q, S if D <= 64 else 128), bf), V((1, S), i32), V((1, S), f32),
            V((D * dcp, F), bf), V((D * dcp, F), bf), V((D, EL, 128), f32), V((D, EL, 128), f32),
            V((EL, R, F), bf), V((EL, R, H), bf), V((EL, R, H), bf), V((EL, R, H), f32),
            V((EL, R, H), f32), V((EL, R, H), bf),
            V((NG, EL, 128), f32), V((NG, ROWS, 128), f32), V((D, EL, 128), f32),
            V((2 * GR, Q), bf), V((D, ROWS, 128), f32), V((D, EL, 128), f32), V((D, EL, 128), f32), V((1, S), f32), V((ROWS, S), f32), V((ROWS, S), f32),
            dma, dma((NCH,)), dma, dma, dma, dma, dma, dma,
        ],
        compiler_params=pltpu.CompilerParams(
            collective_id=0, has_side_effects=True, vmem_limit_bytes=67043328
        ),
    )(
        features, expert_of.reshape(1, S), segment_of, step_len, target, w_first, w_second, w_head
    )
    return pl.pallas_call(
        hand_on,
        out_shape=tuple(jax.ShapeDtypeStruct(o.shape, o.dtype) for o in outs),
        in_specs=[vm] * 4,
        out_specs=(vm,) * 4,
    )(*outs)


def solution(mesh):
    sizes = dict(mesh.shape)
    both = ("expert", "dp")
    three, two = P(both, None, None), P(both, None)
    return jax.shard_map(
        functools.partial(local, sizes["expert"], sizes["dp"]),
        mesh=mesh,
        in_specs=(three, three, two, two, two, three, three, two),
        out_specs=(two, three, three, two),
        check_vma=False,
    )
```

profile of v0, /device:TPU:0, one launch (start us, length us, event | category | flops | bytes accessed | tf_op | source)
XLA Modules:
  0.0 87.9 jit_solution(12016810402338326228)
XLA Ops:
  0.6 85.0 %shard_map.111 = (f32[1,3072]{1,0:T(1,128)}, bf16[4,256,256]{2,1,0:T(8,128)(2,1)}, bf16[4,256,256]{2,1,0:T(8,128)(2,1)}, bf16[4,256]{1,0:T(4,128)(2,1)}) custom-call(bf16[1,3072,256]{2,1,0:T(8,128)(2,1)} %feat.1, s32[1,3072]{1,0:T(1,128)} %bitcast.1, s32[1,3072]{1,0:T(1,128)} %seg.1, f32[1,3072]{1,0:T(1,128)} %step.1, f32[1,3072]{1,0:T(1,128)} %targ.1, ...), custom_call_target="tpu_custom_call" | custom-call | tf_op jit(solution)/shard_map/pallas_call | solution.py:413
  85.6 2.2 %shard_map.112 = (f32[1,3072]{1,0:T(1,128)}, bf16[4,256,256]{2,1,0:T(8,128)(2,1)}, bf16[4,256,256]{2,1,0:T(8,128)(2,1)}, bf16[4,256]{1,0:T(4,128)(2,1)}) custom-call(f32[1,3072]{1,0:T(1,128)} %get-tuple-element.8.refs_0_, bf16[4,256,256]{2,1,0:T(8,128)(2,1)} %get-tuple-element.9.refs_1_, bf16[4,256,256]{2,1,0:T(8,128)(2,1)} %get-tuple-element.10.refs_2_, ...), custom_call_target="tpu_custom_call" | custom-call | tf_op jit(solution)/shard_map/pallas_call | solution.py:438
where the time goes:
time: 88 us; the launch traced here: 87.9 us
  Pallas kernels  87.2 us (99%)
    pallas_call x1, Pallas kernels, local(): pl.pallas_call(functools.partial(kernel, cfg), out_shape=(jax.ShapeDtypeS...  85 us
    pallas_call x1, Pallas kernels, local(): pl.pallas_call(hand_on, out_shape=tuple((jax.ShapeDtypeStruct(o.shape, o....  2.23 us

commit v1 on v0

--- a/solution.py
+++ b/solution.py
@@ -9,6 +9,7 @@
 
 MESH = pl.DeviceIdType.MESH
 ROWS = 8
+PLACE = [('d', 0), ('e', 0), ('d', 1), ('e', 1), ('e', 2)]
 
 
 def up(value, unit):
@@ -39,12 +40,13 @@
 
 def kernel(
     cfg,
-    feat, eof, seg, step, targ, w1, w2, wh,
+    feat_h, eof_h, seg_h, step_h, targ_h, w1_h, w2_h, wh_h,
     ext_o, g1_o, g2_o, gh_o,
+    feat, eof, seg, step, targ, w1, w2, wh, ins,
     own_s, oh_s, slot_s, rank_s,
     send, recv, msend, mrecv,
     x_s, a1_s, a2_s, sl1_s, hs2_s, gp2_s,
-    dens, sig, table, tcol, grads, gsend, grecv, row_s, fore_s, back_s,
+    dens, sig, table, tcol, grads, gsend, grecv, row_s, fore_s, back_s, cf_s, cb_s, acc1, acc2,
     fss, frs, mss, mrs, dss, drs, gss, grs,
 ):
     NE, ND, EL, S, NB, cap, dcp, G, CH = cfg
@@ -56,21 +58,36 @@
     NCH = NG // CH
     CR = CH * GR
     nblk = S // NB
-    lgn = NE.bit_length() - 1
+    H = D // 2
+    le, ld = NE.bit_length() - 1, ND.bit_length() - 1
     keep = D <= 64
     e_me = lax.axis_index("expert")
     d_me = lax.axis_index("dp")
-
-    def shifts(j):
-        return NE - 1 - lax.rem(j, NE), ND - 1 - j // NE
+    spots = [("e", i) for i in range(le)]
+    spots = PLACE if len(PLACE) == le + ld else [("d", i) for i in range(ld)] + spots
+
+    def flips(j, bit, where):
+        mask = where(j < H, H + j, D - 1 - j)
+        ke = [None] * le
+        kd = [None] * ld
+        for i, (axis, w) in enumerate(spots):
+            (ke if axis == "e" else kd)[w] = bit(mask, i)
+        return ke, kd
+
+    def sbit(v, i):
+        return lax.rem(lax.div(v, jnp.int32(1 << i)), jnp.int32(2))
+
+    def vbit(v, i):
+        return (v >> i) & 1
+
+    e_bits = [sbit(e_me, i) for i in range(le)]
+    d_bits = [sbit(d_me, i) for i in range(ld)]
 
     def to_dev(j):
-        ke, kd = shifts(j)
-        return (lax.rem(e_me + ke, NE), lax.rem(d_me + kd, ND))
-
-    def from_dev(j):
-        ke, kd = shifts(j)
-        return (lax.rem(e_me - ke + NE, NE), lax.rem(d_me - kd + ND, ND))
+        ke, kd = flips(j, sbit, jnp.where)
+        e = sum(lax.rem(x + k, jnp.int32(2)) * (1 << i) for i, (x, k) in enumerate(zip(e_bits, ke)))
+        d = sum(lax.rem(x + k, jnp.int32(2)) * (1 << i) for i, (x, k) in enumerate(zip(d_bits, kd)))
+        return (e, d)
 
     barrier = pltpu.get_barrier_semaphore()
 
@@ -79,6 +96,14 @@
         return c
 
     lax.fori_loop(0, D - 1, greet, 0)
+
+    arrays = (
+        (eof_h, eof), (feat_h.at[0], feat), (seg_h, seg), (step_h, step), (targ_h, targ),
+        (w1_h, w1), (w2_h, w2), (wh_h, wh),
+    )
+    loads = [pltpu.make_async_copy(a, b, ins.at[i]) for i, (a, b) in enumerate(arrays)]
+    for load in loads:
+        load.start()
 
     def loop(n, body, init):
         if not keep:
@@ -90,8 +115,9 @@
     qi = lax.broadcasted_iota(jnp.int32, (Q, NB), 0)
     jq = qi >> 3
     mq = qi & (ROWS - 1)
-    de = (e_me + (NE - 1 - (jq & (NE - 1)))) & (NE - 1)
-    dd = (d_me + (ND - 1 - (jq >> lgn))) & (ND - 1)
+    ke, kd = flips(jq, vbit, jnp.where)
+    de = sum(((x + k) & 1) << i for i, (x, k) in enumerate(zip(e_bits, ke)))
+    dd = sum(((x + k) & 1) << i for i, (x, k) in enumerate(zip(d_bits, kd)))
     own_s[...] = jnp.where(mq < EL, (de * ND + dd) * EL + mq, -1)
 
     tri = lax.broadcasted_iota(jnp.int32, (NB, NB + 128), 0) < lax.broadcasted_iota(
@@ -120,6 +146,7 @@
         rank_s[:, cols(b)] = jnp.sum(jnp.where(hit, ranks, 0.0), axis=0, keepdims=True)
         return carry + full[:, NB:]
 
+    loads[0].wait()
     counts = loop(nblk, rank_pass, jnp.zeros((Q, 128), jnp.float32))
     q128 = lax.broadcasted_iota(jnp.int32, (Q, 128), 0)
     ends = counts
@@ -172,7 +199,7 @@
         for b in range(S // 256):
             s = slice(b * 256, (b + 1) * 256)
             want = lax.broadcasted_iota(jnp.int32, (PR, 256), 0)
-            part = nn(one((slot_s[:, s] - p * PR) == want), feat[0, s, :])
+            part = nn(one((slot_s[:, s] - p * PR) == want), feat[s, :])
             acc = part if acc is None else acc + part
         send[pl.ds(pl.multiple_of(p * PR, PR), PR), :] = acc.astype(jnp.bfloat16)
 
@@ -192,21 +219,30 @@
 
         return c
 
+    loads[1].wait()
     lax.fori_loop(0, D // PK, pack_send, 0)
-
-    wide = (ROWS, S)
-    segs = jnp.broadcast_to(seg[...], wide)
+    for load in loads[2:]:
+        load.wait()
+
+    NR = S // 128
+    wide = (NR, 128)
+    segs = seg[...]
     pos = lax.broadcasted_iota(jnp.int32, wide, 1)
+    row = lax.broadcasted_iota(jnp.int32, wide, 0)
     fore = jnp.ones(wide, jnp.float32)
     back = fore
     for k in range(7):
         s = 1 << k
         same = jnp.logical_and(pltpu.roll(segs, s, 1) == segs, pos >= s)
         fore = fore + jnp.where(same, pltpu.roll(fore, s, 1), 0.0)
-        same = jnp.logical_and(pltpu.roll(segs, S - s, 1) == segs, pos < S - s)
-        back = back + jnp.where(same, pltpu.roll(back, S - s, 1), 0.0)
+        same = jnp.logical_and(pltpu.roll(segs, 128 - s, 1) == segs, pos < 128 - s)
+        back = back + jnp.where(same, pltpu.roll(back, 128 - s, 1), 0.0)
     fore_s[...] = fore
     back_s[...] = back
+    ends_of = pltpu.roll(jnp.broadcast_to(segs[:, 127:128], wide), 1, 0)
+    cf_s[...] = jnp.where(jnp.logical_and(ends_of == segs, row > 0), 1.0, 0.0)
+    starts_of = pltpu.roll(jnp.broadcast_to(segs[:, 0:1], wide), NR - 1, 0)
+    cb_s[...] = jnp.where(jnp.logical_and(starts_of == segs, row < NR - 1), 1.0, 0.0)
 
     pltpu.make_async_copy(mrecv, mrecv, mrs).wait()
 
@@ -215,7 +251,8 @@
     lane_j = (lane - lane_g * dcp if G > 1 else lane).astype(jnp.float32)
     sub8 = lax.broadcasted_iota(jnp.int32, (ROWS, 1), 0)
 
-    def forward(ci, c):
+    def forward(i, c):
+        ci = jnp.where(i == 0, 0, jnp.where(i <= NCH // 2, i + NCH // 2 - 1, i - NCH // 2))
         span = pl.ds(pl.multiple_of(ci * SPC * dcp, SPC * dcp), SPC * dcp)
         pltpu.make_async_copy(recv.at[span], recv.at[span], frs.at[ci]).wait()
         for g in range(CH):
@@ -271,7 +308,7 @@
             def _():
                 pltpu.make_async_remote_copy(
                     src_ref=dens.at[j // G], dst_ref=table.at[j], send_sem=dss, recv_sem=drs,
-                    device_id=from_dev(j), device_id_type=MESH,
+                    device_id=to_dev(j), device_id_type=MESH,
                 ).start()
 
             return c2
@@ -289,34 +326,47 @@
     tcol[0:GR, :] = th
     tcol[GR : 2 * GR, :] = tl
 
+    def line(b, t):
+        at = b * (NB // 128) + t
+        return slice(at, at + 1) if keep else pl.ds(at, 1)
+
+    def put(b, x):
+        for t in range(NB // 128):
+            row_s[line(b, t), :] = x[:, t * 128 : (t + 1) * 128]
+
+    def take(b):
+        return jnp.concatenate([row_s[line(b, t), :] for t in range(NB // 128)], axis=1)
+
     def spread(b, c):
         both = nn(tcol[...], hot(b))
         both = both[:GR] + both[GR:]
         want = lax.broadcasted_iota(jnp.int32, (GR, NB), 0).astype(jnp.float32)
-        row_s[:, cols(b)] = jnp.sum(
-            jnp.where(rank_s[:, cols(b)] == want, both, 0.0), axis=0, keepdims=True
-        )
+        put(b, jnp.sum(jnp.where(rank_s[:, cols(b)] == want, both, 0.0), axis=0, keepdims=True))
         return c
 
     loop(nblk, spread, 0)
 
-    steps = jnp.broadcast_to(step[...], wide)
-    run = jnp.broadcast_to(row_s[...], wide) * steps
+    steps = step[...]
+    run = row_s[...] * steps
     before = fore_s[...]
     for k in range(7):
         s = 1 << k
         run = run + jnp.where(before > s, pltpu.roll(run, s, 1), 0.0)
-    ext_o[...] = run[0:1]
-    run = run - jnp.broadcast_to(targ[...], wide)
+    tail = pltpu.roll(jnp.broadcast_to(run[:, 127:128], wide), 1, 0)
+    run = run + jnp.where(cf_s[...] > 0.0, tail, 0.0)
+    ext_o[...] = run
+    run = run - targ[...]
     after = back_s[...]
     for k in range(7):
         s = 1 << k
-        run = run + jnp.where(after > s, pltpu.roll(run, S - s, 1), 0.0)
-    row_s[...] = (run * steps)[0:1]
+        run = run + jnp.where(after > s, pltpu.roll(run, 128 - s, 1), 0.0)
+    head = pltpu.roll(jnp.broadcast_to(run[:, 0:1], wide), NR - 1, 0)
+    run = run + jnp.where(cb_s[...] > 0.0, head, 0.0)
+    row_s[...] = run * steps
 
     def collect(b, total):
         want = lax.broadcasted_iota(jnp.int32, (GR, NB), 0).astype(jnp.float32)
-        held = jnp.where(rank_s[:, cols(b)] == want, row_s[:, cols(b)], 0.0)
+        held = jnp.where(rank_s[:, cols(b)] == want, take(b), 0.0)
         both = jnp.concatenate(split2(held), axis=0)
         return total + nt(hot(b), both)
 
@@ -325,57 +375,58 @@
     got = jnp.concatenate([got, jnp.zeros((Q, 128 - GR), jnp.float32)], axis=1)
     gsend[...] = got.reshape(D, ROWS, 128)[:, :EL, :]
 
-    pltpu.make_async_copy(gsend.at[D - 1], grecv.at[D - 1], grs).start()
-
     def grad_copy(j, c):
         pltpu.make_async_remote_copy(
-            src_ref=gsend.at[j], dst_ref=grecv.at[j], send_sem=gss, recv_sem=grs,
+            src_ref=gsend.at[j], dst_ref=grecv.at[j], send_sem=gss, recv_sem=grs.at[j // H],
             device_id=to_dev(j), device_id_type=MESH,
         ).start()
         return c
 
-    lax.fori_loop(0, D - 1, grad_copy, 0)
-    pltpu.make_async_copy(grecv, grecv, grs).wait()
-
-    wid = w1.shape[2]
-
-    def scale(ci, accs):
-        parts = []
-        for g in range(CH):
-            grp = ci * CH + g
-            tot = grecv[grp * G]
-            for h in range(1, G):
-                tot = tot + grecv[grp * G + h]
-            parts.append(jnp.concatenate([tot, tot], axis=0)[:ROWS] * sig[grp])
-        gt = jnp.concatenate(parts, axis=0).T[:GR]
-        out = []
+    lax.fori_loop(0, H, lambda j, c: grad_copy(H - 1 - j, c), 0)
+    lax.fori_loop(H, D - 1, grad_copy, 0)
+    pltpu.make_async_copy(gsend.at[D - 1], grecv.at[D - 1], grs.at[1]).start()
+
+    RH = NG * GR // 2
+
+    def backward(h, heads):
+        got = grecv.at[pl.ds(h * H, H)]
+        pltpu.make_async_copy(got, got, grs.at[h]).wait()
+        for ci in range(h * NCH // 2, (h + 1) * NCH // 2):
+            parts = []
+            for g in range(CH):
+                grp = ci * CH + g
+                tot = grecv[grp * G]
+                for t in range(1, G):
+                    tot = tot + grecv[grp * G + t]
+                parts.append(jnp.concatenate([tot, tot], axis=0)[:ROWS] * sig[grp])
+            gt = jnp.concatenate(parts, axis=0).T[:GR]
+            gb = jnp.concatenate([p[:, :GR] for p in parts], axis=1)
+            gb = jnp.concatenate([gb, gb], axis=0).astype(jnp.bfloat16)
+            for e in range(EL):
+                for g in range(CH):
+                    at = (ci * CH + g) * GR
+                    rows = slice(at, at + GR)
+                    q = g * ROWS + e
+                    gp2_s[e, rows, :] = (gt[:, q : q + 1] * hs2_s[e, rows, :]).astype(jnp.bfloat16)
+                heads[e] = heads[e] + nn(gb, a2_s[e, ci * CR : (ci + 1) * CR, :])
+        half = slice(h * RH, (h + 1) * RH)
         for e in range(EL):
-            acc = accs[e]
-            for g in range(CH):
-                rows = pl.ds(pl.multiple_of((ci * CH + g) * GR, GR), GR)
-                q = g * ROWS + e
-                col = gt[:, q : q + 1]
-                gp2_s[e, rows, :] = (col * hs2_s[e, rows, :]).astype(jnp.bfloat16)
-                colb = col.astype(jnp.bfloat16).astype(jnp.float32)
-                acc = acc + colb * a2_s[e, rows, :].astype(jnp.float32)
-            out.append(acc)
-        return tuple(out)
-
-    accs = lax.fori_loop(
-        0, NCH, scale, tuple(jnp.zeros((GR, wid), jnp.float32) for _ in range(EL))
-    )
+            gp2 = gp2_s[e, half, :]
+            d2 = tn(a1_s[e, half, :], gp2)
+            gp1 = (nt(gp2, w2[e]) * sl1_s[e, half, :]).astype(jnp.bfloat16)
+            d1 = tn(x_s[e, half, :], gp1)
+            if h:
+                acc2[e] = d2
+                acc1[e] = d1
+            else:
+                g2_o[e] = (acc2[e] + d2).astype(jnp.bfloat16)
+                g1_o[e] = (acc1[e] + d1).astype(jnp.bfloat16)
+        return heads
+
+    heads = [jnp.zeros((2 * ROWS, w1.shape[2]), jnp.float32) for _ in range(EL)]
+    heads = backward(0, backward(1, heads))
     for e in range(EL):
-        gh_o[e : e + 1, :] = jnp.sum(accs[e], axis=0, keepdims=True).astype(jnp.bfloat16)
-
-    def weights(e, c):
-        gp2 = gp2_s[e]
-        g2_o[e] = tn(a1_s[e], gp2).astype(jnp.bfloat16)
-        gp1 = (nt(gp2, w2[e]) * sl1_s[e]).astype(jnp.bfloat16)
-        g1_o[e] = tn(x_s[e], gp1).astype(jnp.bfloat16)
-        return c
-
-    for e in range(EL):
-        weights(e, 0)
+        gh_o[e : e + 1, :] = heads[e][e : e + 1].astype(jnp.bfloat16)
 
     sent = pl.ds(0, (D - 1) * dcp)
     pltpu.make_async_copy(send.at[sent], send.at[sent], fss).wait()
@@ -409,38 +460,45 @@
     V = pltpu.VMEM
     dma = pltpu.SemaphoreType.DMA
     R = NG * GR
+    NR = S // 128
+    rows = (NR, 128)
     vm = pl.BlockSpec(memory_space=pltpu.VMEM)
     outs = pl.pallas_call(
         functools.partial(kernel, cfg),
         out_shape=(
-            jax.ShapeDtypeStruct((1, S), f32),
+            jax.ShapeDtypeStruct((NR, 128), f32),
             jax.ShapeDtypeStruct((EL, F, H), bf),
             jax.ShapeDtypeStruct((EL, H, H), bf),
             jax.ShapeDtypeStruct((EL, H), bf),
         ),
-        in_specs=[vm] * 8,
+        in_specs=[pl.BlockSpec(memory_space=pl.ANY)] * 8,
         out_specs=(vm,) * 4,
         scratch_shapes=[
+            V((S, F), bf), V((1, S), i32), V(rows, i32), V(rows, f32), V(rows, f32),
+            V((EL, F, H), bf), V((EL, H, H), bf), V((EL, H), bf), dma((8,)),
             V((Q, NB), i32), V((Q, S if D <= 64 else 128), bf), V((1, S), i32), V((1, S), f32),
             V((D * dcp, F), bf), V((D * dcp, F), bf), V((D, EL, 128), f32), V((D, EL, 128), f32),
             V((EL, R, F), bf), V((EL, R, H), bf), V((EL, R, H), bf), V((EL, R, H), f32),
             V((EL, R, H), f32), V((EL, R, H), bf),
             V((NG, EL, 128), f32), V((NG, ROWS, 128), f32), V((D, EL, 128), f32),
-            V((2 * GR, Q), bf), V((D, ROWS, 128), f32), V((D, EL, 128), f32), V((D, EL, 128), f32), V((1, S), f32), V((ROWS, S), f32), V((ROWS, S), f32),
-            dma, dma((NCH,)), dma, dma, dma, dma, dma, dma,
+            V((2 * GR, Q), bf), V((D, ROWS, 128), f32), V((D, EL, 128), f32), V((D, EL, 128), f32), V(rows, f32), V(rows, f32), V(rows, f32),
+            V(rows, f32), V(rows, f32), V((EL, F, H), f32), V((EL, H, H), f32),
+            dma, dma((NCH,)), dma, dma, dma, dma, dma, dma((2,)),
         ],
         compiler_params=pltpu.CompilerParams(
             collective_id=0, has_side_effects=True, vmem_limit_bytes=67043328
         ),
     )(
-        features, expert_of.reshape(1, S), segment_of, step_len, target, w_first, w_second, w_head
+        features, expert_of.reshape(1, S), segment_of.reshape(rows), step_len.reshape(rows),
+        target.reshape(rows), w_first, w_second, w_head
     )
-    return pl.pallas_call(
+    ext, *grads = pl.pallas_call(
         hand_on,
         out_shape=tuple(jax.ShapeDtypeStruct(o.shape, o.dtype) for o in outs),
         in_specs=[vm] * 4,
         out_specs=(vm,) * 4,
     )(*outs)
+    return ext.reshape(1, S), *grads
 
 
 def solution(mesh):

time: 88 us -> 83.4 us (0.948)
  Pallas kernels: 87.2 us -> 82.5 us
    pallas_call x1, Pallas kernels: 85 us -> 80.3 us  [local(): pl.pallas_call(functools.partial(kernel, cfg), out_shape=(jax.ShapeDtypeS...]
where the time goes in v1:
time: 83.4 us; the launch traced here: 83.2 us
  Pallas kernels  82.5 us (99%)
    pallas_call x1, Pallas kernels, local(): pl.pallas_call(functools.partial(kernel, cfg), out_shape=(jax.ShapeDtypeS...  80.3 us
    pallas_call x1, Pallas kernels, local(): pl.pallas_call(hand_on, out_shape=tuple((jax.ShapeDtypeStruct(o.shape, o....  2.23 us

profile of v1, /device:TPU:0, one launch (start us, length us, event | category | flops | bytes accessed | tf_op | source)
XLA Modules:
  0.0 83.2 jit_solution(14302540198020387698)
XLA Ops:
  0.6 80.3 %shard_map.111 = (f32[24,128]{1,0:T(8,128)}, bf16[4,256,256]{2,1,0:T(8,128)(2,1)}, bf16[4,256,256]{2,1,0:T(8,128)(2,1)}, bf16[4,256]{1,0:T(4,128)(2,1)}) custom-call(bf16[1,3072,256]{2,1,0:T(8,128)(2,1)} %feat_h.1, s32[1,3072]{1,0:T(1,128)} %bitcast.5, s32[24,128]{1,0:T(8,128)} %bitcast.6, f32[24,128]{1,0:T(8,128)} %bitcast.7, f32[24,128]{1,0:T(8,128)} %bitcast.8, ...), custom_call_target="tpu_custom_call" | custom-call | tf_op jit(solution)/shard_map/pallas_call | solution.py:466
  80.9 2.2 %shard_map.112 = (f32[24,128]{1,0:T(8,128)}, bf16[4,256,256]{2,1,0:T(8,128)(2,1)}, bf16[4,256,256]{2,1,0:T(8,128)(2,1)}, bf16[4,256]{1,0:T(4,128)(2,1)}) custom-call(f32[24,128]{1,0:T(8,128)} %get-tuple-element.12.refs_0_, bf16[4,256,256]{2,1,0:T(8,128)(2,1)} %get-tuple-element.13.refs_1_, bf16[4,256,256]{2,1,0:T(8,128)(2,1)} %get-tuple-element.14.refs_2_, ...), custom_call_target="tpu_custom_call" | custom-call | tf_op jit(solution)/shard_map/pallas_call | solution.py:495

commit v2 on v1

--- a/solution.py
+++ b/solution.py
@@ -9,6 +9,8 @@
 
 MESH = pl.DeviceIdType.MESH
 ROWS = 8
+STEPS = ((1, 4), (4, 4), (16, 4), (64, 2))
+ORDER = (6, 7, 4, 0, 1, 5, 2, 3)
 PLACE = [('d', 0), ('e', 0), ('d', 1), ('e', 1), ('e', 2)]
 
 
@@ -45,7 +47,7 @@
     feat, eof, seg, step, targ, w1, w2, wh, ins,
     own_s, oh_s, slot_s, rank_s,
     send, recv, msend, mrecv,
-    x_s, a1_s, a2_s, sl1_s, hs2_s, gp2_s,
+    x_s, a1_s, a2_s, sl1_s, hs2_s, gp2_s, gp1_s,
     dens, sig, table, tcol, grads, gsend, grecv, row_s, fore_s, back_s, cf_s, cb_s, acc1, acc2,
     fss, frs, mss, mrs, dss, drs, gss, grs,
 ):
@@ -251,8 +253,16 @@
     lane_j = (lane - lane_g * dcp if G > 1 else lane).astype(jnp.float32)
     sub8 = lax.broadcasted_iota(jnp.int32, (ROWS, 1), 0)
 
+    def chunk_at(i):
+        part = max(NCH // 8, 1)
+        block = lax.div(i, jnp.int32(part))
+        at = jnp.int32(ORDER[0] if NCH >= 8 else 0)
+        for k, v in enumerate(ORDER):
+            at = jnp.where(block == k, v, at)
+        return at * part + lax.rem(i, jnp.int32(part)) if NCH >= 8 else i
+
     def forward(i, c):
-        ci = jnp.where(i == 0, 0, jnp.where(i <= NCH // 2, i + NCH // 2 - 1, i - NCH // 2))
+        ci = chunk_at(i)
         span = pl.ds(pl.multiple_of(ci * SPC * dcp, SPC * dcp), SPC * dcp)
         pltpu.make_async_copy(recv.at[span], recv.at[span], frs.at[ci]).wait()
         for g in range(CH):
@@ -316,7 +326,22 @@
         lax.fori_loop(ci * SPC, (ci + 1) * SPC, give, 0)
         return c
 
-    lax.fori_loop(0, NCH, forward, 0)
+    RH = NG * GR // 2
+
+    def prepare(h):
+        half = slice(h * RH, (h + 1) * RH)
+        for e in range(EL):
+            back_one = nt(hs2_s[e, half, :].astype(jnp.bfloat16), w2[e])
+            sl1_s[e, half, :] = sl1_s[e, half, :] * back_one
+
+    last = 2 * max(NCH // 8, 1) if NCH >= 8 else 0
+    lax.fori_loop(0, NCH - last, forward, 0)
+    if last:
+        prepare(1)
+        lax.fori_loop(NCH - last, NCH, forward, 0)
+    else:
+        prepare(1)
+    prepare(0)
 
     grads[...] = jnp.zeros_like(grads)
     pltpu.make_async_copy(table, table, drs).wait()
@@ -349,17 +374,19 @@
     steps = step[...]
     run = row_s[...] * steps
     before = fore_s[...]
-    for k in range(7):
-        s = 1 << k
-        run = run + jnp.where(before > s, pltpu.roll(run, s, 1), 0.0)
+    for s, times in STEPS:
+        run = run + sum(
+            jnp.where(before > t * s, pltpu.roll(run, t * s, 1), 0.0) for t in range(1, times)
+        )
     tail = pltpu.roll(jnp.broadcast_to(run[:, 127:128], wide), 1, 0)
     run = run + jnp.where(cf_s[...] > 0.0, tail, 0.0)
     ext_o[...] = run
     run = run - targ[...]
     after = back_s[...]
-    for k in range(7):
-        s = 1 << k
-        run = run + jnp.where(after > s, pltpu.roll(run, 128 - s, 1), 0.0)
+    for s, times in STEPS:
+        run = run + sum(
+            jnp.where(after > t * s, pltpu.roll(run, 128 - t * s, 1), 0.0) for t in range(1, times)
+        )
     head = pltpu.roll(jnp.broadcast_to(run[:, 0:1], wide), NR - 1, 0)
     run = run + jnp.where(cb_s[...] > 0.0, head, 0.0)
     row_s[...] = run * steps
@@ -385,8 +412,6 @@
     lax.fori_loop(0, H, lambda j, c: grad_copy(H - 1 - j, c), 0)
     lax.fori_loop(H, D - 1, grad_copy, 0)
     pltpu.make_async_copy(gsend.at[D - 1], grecv.at[D - 1], grs.at[1]).start()
-
-    RH = NG * GR // 2
 
     def backward(h, heads):
         got = grecv.at[pl.ds(h * H, H)]
@@ -407,14 +432,14 @@
                     at = (ci * CH + g) * GR
                     rows = slice(at, at + GR)
                     q = g * ROWS + e
-                    gp2_s[e, rows, :] = (gt[:, q : q + 1] * hs2_s[e, rows, :]).astype(jnp.bfloat16)
+                    col = gt[:, q : q + 1]
+                    gp2_s[e, rows, :] = (col * hs2_s[e, rows, :]).astype(jnp.bfloat16)
+                    gp1_s[e, rows, :] = (col * sl1_s[e, rows, :]).astype(jnp.bfloat16)
                 heads[e] = heads[e] + nn(gb, a2_s[e, ci * CR : (ci + 1) * CR, :])
         half = slice(h * RH, (h + 1) * RH)
         for e in range(EL):
-            gp2 = gp2_s[e, half, :]
-            d2 = tn(a1_s[e, half, :], gp2)
-            gp1 = (nt(gp2, w2[e]) * sl1_s[e, half, :]).astype(jnp.bfloat16)
-            d1 = tn(x_s[e, half, :], gp1)
+            d2 = tn(a1_s[e, half, :], gp2_s[e, half, :])
+            d1 = tn(x_s[e, half, :], gp1_s[e, half, :])
             if h:
                 acc2[e] = d2
                 acc1[e] = d1
@@ -437,9 +462,16 @@
 
 
 def hand_on(*refs):
+    *refs, sems = refs
     half = len(refs) // 2
-    for source, to in zip(refs[:half], refs[half:]):
-        to[...] = source[...]
+    copies = [
+        pltpu.make_async_copy(source, to, sems.at[i])
+        for i, (source, to) in enumerate(zip(refs[:half], refs[half:]))
+    ]
+    for copy in copies:
+        copy.start()
+    for copy in copies:
+        copy.wait()
 
 
 def local(ne, nd, features, expert_of, segment_of, step_len, target, w_first, w_second, w_head):
@@ -450,7 +482,7 @@
     dcp = up(3 * cap, 16)
     G = 1 if cap % 16 == 0 else 16
     NG = D // G
-    CH = 4 if NG % 4 == 0 else 1
+    CH = 2 if NG % 16 == 0 else 1
     NCH = NG // CH
     NB = 256 if D <= 64 else 128
     GR = G * cap
@@ -471,7 +503,7 @@
             jax.ShapeDtypeStruct((EL, H, H), bf),
             jax.ShapeDtypeStruct((EL, H), bf),
         ),
-        in_specs=[pl.BlockSpec(memory_space=pl.ANY)] * 8,
+        in_specs=[pl.BlockSpec(memory_space=pltpu.HBM)] * 8,
         out_specs=(vm,) * 4,
         scratch_shapes=[
             V((S, F), bf), V((1, S), i32), V(rows, i32), V(rows, f32), V(rows, f32),
@@ -479,24 +511,26 @@
             V((Q, NB), i32), V((Q, S if D <= 64 else 128), bf), V((1, S), i32), V((1, S), f32),
             V((D * dcp, F), bf), V((D * dcp, F), bf), V((D, EL, 128), f32), V((D, EL, 128), f32),
             V((EL, R, F), bf), V((EL, R, H), bf), V((EL, R, H), bf), V((EL, R, H), f32),
-            V((EL, R, H), f32), V((EL, R, H), bf),
+            V((EL, R, H), f32), V((EL, R, H), bf), V((EL, R, H), bf),
             V((NG, EL, 128), f32), V((NG, ROWS, 128), f32), V((D, EL, 128), f32),
             V((2 * GR, Q), bf), V((D, ROWS, 128), f32), V((D, EL, 128), f32), V((D, EL, 128), f32), V(rows, f32), V(rows, f32), V(rows, f32),
             V(rows, f32), V(rows, f32), V((EL, F, H), f32), V((EL, H, H), f32),
             dma, dma((NCH,)), dma, dma, dma, dma, dma, dma((2,)),
         ],
         compiler_params=pltpu.CompilerParams(
-            collective_id=0, has_side_effects=True, vmem_limit_bytes=67043328
+            collective_id=0, has_side_effects=True, vmem_limit_bytes=52 * 1024 * 1024
         ),
     )(
-        features, expert_of.reshape(1, S), segment_of.reshape(rows), step_len.reshape(rows),
-        target.reshape(rows), w_first, w_second, w_head
+        *[pltpu.with_memory_space_constraint(x, pltpu.HBM) for x in (features, expert_of.reshape(1, S), segment_of.reshape(rows), step_len.reshape(rows),
+        target.reshape(rows), w_first, w_second, w_head)]
     )
     ext, *grads = pl.pallas_call(
         hand_on,
         out_shape=tuple(jax.ShapeDtypeStruct(o.shape, o.dtype) for o in outs),
         in_specs=[vm] * 4,
-        out_specs=(vm,) * 4,
+        out_specs=(pl.BlockSpec(memory_space=pltpu.HBM),) * 4,
+        scratch_shapes=[dma((4,))],
+        compiler_params=pltpu.CompilerParams(vmem_limit_bytes=4 * 1024 * 1024),
     )(*outs)
     return ext.reshape(1, S), *grads
 

time: 83.4 us -> 79 us (0.947)
  Pallas kernels: 82.5 us -> 78.1 us
    pallas_call x1, Pallas kernels: 80.3 us -> 77.1 us  [local(): pl.pallas_call(functools.partial(kernel, cfg), out_shape=(jax.ShapeDtypeS...]
    pallas_call x1, Pallas kernels: 2.23 us -> 1.01 us  [local(): pl.pallas_call(hand_on, out_shape=tuple((jax.ShapeDtypeStruct(o.shape, o....]
where the time goes in v2:
time: 79 us; the launch traced here: 78.8 us
  Pallas kernels  78.1 us (99%)
    pallas_call x1, Pallas kernels, local(): pl.pallas_call(functools.partial(kernel, cfg), out_shape=(jax.ShapeDtypeS...  77.1 us

profile of v2, /device:TPU:0, one launch (start us, length us, event | category | flops | bytes accessed | tf_op | source)
XLA Modules:
  0.0 78.8 jit_solution(7372347775060458818)
XLA Ops:
  0.6 77.1 %shard_map.111 = (f32[24,128]{1,0:T(8,128)S(1)}, bf16[4,256,256]{2,1,0:T(8,128)(2,1)S(1)}, bf16[4,256,256]{2,1,0:T(8,128)(2,1)S(1)}, bf16[4,256]{1,0:T(4,128)(2,1)S(1)}) custom-call(bf16[1,3072,256]{2,1,0:T(8,128)(2,1)} %feat_h.1, s32[1,3072]{1,0:T(1,128)} %bitcast.5, s32[24,128]{1,0:T(8,128)} %bitcast.6, f32[24,128]{1,0:T(8,128)} %bitcast.7, ...), custom_call_target="tpu_custom_call" | custom-call | tf_op jit(solution)/shard_map/pallas_call | solution.py:498
  77.7 1.0 %shard_map.112 = (f32[24,128]{1,0:T(8,128)}, bf16[4,256,256]{2,1,0:T(8,128)(2,1)}, bf16[4,256,256]{2,1,0:T(8,128)(2,1)}, bf16[4,256]{1,0:T(4,128)(2,1)}) custom-call(f32[24,128]{1,0:T(8,128)S(1)} %get-tuple-element.12.refs_0_, bf16[4,256,256]{2,1,0:T(8,128)(2,1)S(1)} %get-tuple-element.13.refs_1_, bf16[4,256,256]{2,1,0:T(8,128)(2,1)S(1)} %get-tuple-element.14.refs_2_, ...), custom_call_target="tpu_custom_call" | custom-call | tf_op jit(solution)/shard_map/pallas_call | solution.py:527

commit v3 on v2

--- a/solution.py
+++ b/solution.py
@@ -9,6 +9,7 @@
 
 MESH = pl.DeviceIdType.MESH
 ROWS = 8
+EARLY = 1
 STEPS = ((1, 4), (4, 4), (16, 4), (64, 2))
 ORDER = (6, 7, 4, 0, 1, 5, 2, 3)
 PLACE = [('d', 0), ('e', 0), ('d', 1), ('e', 1), ('e', 2)]
@@ -86,6 +87,14 @@
     d_bits = [sbit(d_me, i) for i in range(ld)]
 
     def to_dev(j):
+        if isinstance(j, int):
+            mask = H + j if j < H else D - 1 - j
+            e, d = jnp.int32(0), jnp.int32(0)
+            for i, (axis, w) in enumerate(spots):
+                bit = (e_bits if axis == "e" else d_bits)[w]
+                bit = (1 - bit if mask >> i & 1 else bit) * (1 << w)
+                e, d = (e + bit, d) if axis == "e" else (e, d + bit)
+            return (e, d)
         ke, kd = flips(j, sbit, jnp.where)
         e = sum(lax.rem(x + k, jnp.int32(2)) * (1 << i) for i, (x, k) in enumerate(zip(e_bits, ke)))
         d = sum(lax.rem(x + k, jnp.int32(2)) * (1 << i) for i, (x, k) in enumerate(zip(d_bits, kd)))
@@ -93,11 +102,18 @@
 
     barrier = pltpu.get_barrier_semaphore()
 
-    def greet(j, c):
+    def each(low, high, f):
+        if keep:
+            for j in range(low, high):
+                f(j)
+        else:
+            lax.fori_loop(low, high, lambda j, c: (f(j), c)[1], 0)
+
+    def greet(j):
         pl.semaphore_signal(barrier, inc=1, device_id=to_dev(j), device_id_type=MESH)
-        return c
-
-    lax.fori_loop(0, D - 1, greet, 0)
+
+    each(0, H, lambda j: greet(H - 1 - j))
+    each(H, D - 1, greet)
 
     arrays = (
         (eof_h, eof), (feat_h.at[0], feat), (seg_h, seg), (step_h, step), (targ_h, targ),
@@ -171,20 +187,11 @@
 
     loop(nblk, slot_pass, 0)
 
-    pl.semaphore_wait(barrier, D - 1)
+    PK = 2
+    PR = PK * dcp
 
     def frows(j):
-        return pl.ds(pl.multiple_of(j * dcp, dcp), dcp)
-
-    def meta_copy(j, c):
-        pltpu.make_async_remote_copy(
-            src_ref=msend.at[j], dst_ref=mrecv.at[j], send_sem=mss, recv_sem=mrs,
-            device_id=to_dev(j), device_id_type=MESH,
-        ).start()
-        return c
-
-    lax.fori_loop(0, D - 1, meta_copy, 0)
-    pltpu.make_async_copy(msend.at[D - 1], mrecv.at[D - 1], mrs).start()
+        return pl.ds(j * dcp if isinstance(j, int) else pl.multiple_of(j * dcp, dcp), dcp)
 
     def feature_copy(j):
         pltpu.make_async_remote_copy(
@@ -193,8 +200,11 @@
             device_id=to_dev(j), device_id_type=MESH,
         ).start()
 
-    PK = 2
-    PR = PK * dcp
+    def meta_copy(j):
+        pltpu.make_async_remote_copy(
+            src_ref=msend.at[j], dst_ref=mrecv.at[j], send_sem=mss, recv_sem=mrs,
+            device_id=to_dev(j), device_id_type=MESH,
+        ).start()
 
     def pack(p):
         acc = None
@@ -207,22 +217,22 @@
 
     def pack_send(p, c):
         pack(p)
-
         feature_copy(p * PK)
-
-        @pl.when(p < D // PK - 1)
-        def _():
-            feature_copy(p * PK + 1)
-
-        @pl.when(p == D // PK - 1)
-        def _():
-            mine = frows(D - 1)
-            pltpu.make_async_copy(send.at[mine], recv.at[mine], frs.at[NCH - 1]).start()
-
+        feature_copy(p * PK + 1)
         return c
 
     loads[1].wait()
-    lax.fori_loop(0, D // PK, pack_send, 0)
+    lax.fori_loop(0, EARLY, lambda p, c: (pack(p), c)[1], 0)
+    pl.semaphore_wait(barrier, D - 1)
+    each(0, D - 1, meta_copy)
+    pltpu.make_async_copy(msend.at[D - 1], mrecv.at[D - 1], mrs).start()
+    for j in range(EARLY * PK):
+        feature_copy(j)
+    lax.fori_loop(EARLY, D // PK - 1, pack_send, 0)
+    pack(jnp.int32(D // PK - 1))
+    feature_copy(D - 2)
+    mine = frows(D - 1)
+    pltpu.make_async_copy(send.at[mine], recv.at[mine], frs.at[NCH - 1]).start()
     for load in loads[2:]:
         load.wait()
 
@@ -402,15 +412,14 @@
     got = jnp.concatenate([got, jnp.zeros((Q, 128 - GR), jnp.float32)], axis=1)
     gsend[...] = got.reshape(D, ROWS, 128)[:, :EL, :]
 
-    def grad_copy(j, c):
+    def grad_copy(j):
         pltpu.make_async_remote_copy(
             src_ref=gsend.at[j], dst_ref=grecv.at[j], send_sem=gss, recv_sem=grs.at[j // H],
             device_id=to_dev(j), device_id_type=MESH,
         ).start()
-        return c
-
-    lax.fori_loop(0, H, lambda j, c: grad_copy(H - 1 - j, c), 0)
-    lax.fori_loop(H, D - 1, grad_copy, 0)
+
+    each(0, H, lambda j: grad_copy(H - 1 - j))
+    each(H, D - 1, grad_copy)
     pltpu.make_async_copy(gsend.at[D - 1], grecv.at[D - 1], grs.at[1]).start()
 
     def backward(h, heads):

time: 79 us -> 77.4 us (0.980)
  Pallas kernels: 78.1 us -> 76.5 us
    pallas_call x1, Pallas kernels: 77.1 us -> 75.5 us  [local(): pl.pallas_call(functools.partial(kernel, cfg), out_shape=(jax.ShapeDtypeS...]
where the time goes in v3:
time: 77.4 us; the launch traced here: 77.2 us
  Pallas kernels  76.5 us (99%)
    pallas_call x1, Pallas kernels, local(): pl.pallas_call(functools.partial(kernel, cfg), out_shape=(jax.ShapeDtypeS...  75.5 us

profile of v3, /device:TPU:0, one launch (start us, length us, event | category | flops | bytes accessed | tf_op | source)
XLA Modules:
  0.0 77.2 jit_solution(3953334659733716767)
XLA Ops:
  0.6 75.5 %shard_map.111 = (f32[24,128]{1,0:T(8,128)S(1)}, bf16[4,256,256]{2,1,0:T(8,128)(2,1)S(1)}, bf16[4,256,256]{2,1,0:T(8,128)(2,1)S(1)}, bf16[4,256]{1,0:T(4,128)(2,1)S(1)}) custom-call(bf16[1,3072,256]{2,1,0:T(8,128)(2,1)} %feat_h.1, s32[1,3072]{1,0:T(1,128)} %bitcast.5, s32[24,128]{1,0:T(8,128)} %bitcast.6, f32[24,128]{1,0:T(8,128)} %bitcast.7, ...), custom_call_target="tpu_custom_call" | custom-call | tf_op jit(solution)/shard_map/pallas_call | solution.py:507
  76.2 1.0 %shard_map.112 = (f32[24,128]{1,0:T(8,128)}, bf16[4,256,256]{2,1,0:T(8,128)(2,1)}, bf16[4,256,256]{2,1,0:T(8,128)(2,1)}, bf16[4,256]{1,0:T(4,128)(2,1)}) custom-call(f32[24,128]{1,0:T(8,128)S(1)} %get-tuple-element.12.refs_0_, bf16[4,256,256]{2,1,0:T(8,128)(2,1)S(1)} %get-tuple-element.13.refs_1_, bf16[4,256,256]{2,1,0:T(8,128)(2,1)S(1)} %get-tuple-element.14.refs_2_, ...), custom_call_target="tpu_custom_call" | custom-call | tf_op jit(solution)/shard_map/pallas_call | solution.py:536
